TPU v7x, 32 devices: a whole 2x2x4 slice. The times are simulated.
32 devices in a mesh: grp: 16 (over z, y, core), sub: 2 (over x).
Axes of the slice: x: 2, y: 2, z: 4, core: 2. Of those that a mesh axis runs over, the one named last changes fastest.
Arguments:
- displacement: float32 [128, 32, 256], P('grp', 'sub'), may hold values from -2 to 2
- load: float32 [128, 32, 256], P('grp', 'sub'), may hold values from -6 to 6
- kl_coef: float32 [32], replicated, may hold values from -3 to 3
- damaged: int32 [16], replicated, may hold values from 0 to 1048575, as said below
- owner: int32 [16], replicated, may hold values from 0 to 15, each once
- phase: float32 [16, 32, 1024], P('grp', 'sub'), may hold values from 1 to 10
- soften: float32 [16, 32, 1024], P('grp', 'sub'), may hold values from 0.5 to 4
Outputs:
- step_field: float32 [128, 32, 256], P('grp', 'sub')
- residual: float32 [128, 32, 256], P('grp', 'sub')
- tangents: float32 [16, 9], replicated
- point_flux: float32 [16, 3], replicated
Inputs may be any that keep to these rules, and one draw needn't show every extreme that they name: `damaged`: point p lies in rows p * 8 to (p + 1) * 8 - 1 of the first dimension, so the points are distinct cells. `owner`: each periodic cell resolves exactly one damaged point.
All inputs are finite; a program needn't handle non-finite values.
Results may differ from a plain program's by a relative error of at most 0.00045.
Values sent between devices are 32-bit elements; how exact they have to be, the bound alone decides.
A program may use at most 320 MiB of HBM per device.

v0:
```python
import jax
import jax.numpy as jnp
from jax import lax
from jax.sharding import PartitionSpec as P

M = 32
MITERS = 4
CG_ITERS = 6
K0 = 6.0
SHIFT = 0.002
HIGH = lax.Precision.HIGHEST


def extended(block, sides, width):
    for axis, dim in sides:
        count = lax.axis_size(axis)
        forward = [(i, i + 1) for i in range(count - 1)]
        backward = [(target, source) for source, target in forward]
        low = lax.ppermute(
            lax.slice_in_dim(block, block.shape[dim] - width, None, axis=dim), axis, forward
        )
        high = lax.ppermute(lax.slice_in_dim(block, 0, width, axis=dim), axis, backward)
        block = jnp.concatenate([low, block, high], axis=dim)
    return block


def passed_along(x, axis, by):
    size = lax.axis_size(axis)
    return lax.ppermute(x, axis, [(i, (i + by) % size) for i in range(size)])


def conductivity(kl_coef, xs, ys, zs, total_x, total_y, total_z):
    order = jnp.arange(4, dtype=jnp.float32)[:, None] + 1.0
    base_x = jnp.cos(jnp.pi * order * (xs.astype(jnp.float32)[None] + 0.5) / total_x)
    base_y = jnp.cos(jnp.pi * order * (ys.astype(jnp.float32)[None] + 0.5) / total_y)
    base_z = jnp.cos(jnp.pi * order[:2] * (zs.astype(jnp.float32)[None] + 0.5) / total_z)
    coef = kl_coef.reshape(2, 4, 4)
    field = jnp.einsum("cba,ai,bj,ck->ijk", coef, base_x, base_y, base_z, precision=HIGH)
    return jnp.exp(0.4 * field)


def padded_gradient(field):
    padded = extended(field, (("grp", 0), ("sub", 1)), 1)
    center = padded[:-1, :-1]
    beyond = jnp.concatenate([center[:, :, 1:], jnp.zeros_like(center[:, :, :1])], 2)
    return jnp.stack([padded[1:, :-1] - center, padded[:-1, 1:] - center, beyond - center])


def point_values(grads, flat, in_cells):
    picked = grads.reshape(3, -1)[:, flat]
    local_part = jnp.where(in_cells[None], picked, 0.0).T
    return lax.psum(local_part, ("grp", "sub"))


def divergence(grads, field, kpad, tensors, flat, target):
    flux = kpad[None] * grads
    picked = grads.reshape(3, -1)[:, flat]
    newval = jnp.einsum("pij,jp->ip", tensors, picked, precision=HIGH)
    flux = flux.reshape(3, -1).at[:, target].set(newval, mode="drop").reshape(grads.shape)
    upper_z = flux[2, 1:, 1:]
    lower_z = jnp.pad(upper_z[:, :, :-1], ((0, 0), (0, 0), (1, 0)))
    out = (
        flux[0, :-1, 1:] - flux[0, 1:, 1:] + flux[1, 1:, :-1] - flux[1, 1:, 1:] + lower_z - upper_z
    )
    return out + SHIFT * field


def along_cols(field, table, letter):
    shape = field.shape
    square = field.reshape(shape[:-1] + (M, M))
    if letter == "z":
        result = jnp.einsum("cpyz,zw->cpyw", square, table, precision=HIGH)
    else:
        result = jnp.einsum("cpyz,yw->cpwz", square, table, precision=HIGH)
    return result.reshape(shape)


def along_planes(field, table):
    return jnp.einsum("cxk,xw->cwk", field, table, precision=HIGH)


def tables_for(size):
    freq = jnp.arange(size, dtype=jnp.int32)
    angle = 2.0 * jnp.pi * (freq[:, None] * freq[None, :] % size).astype(jnp.float32) / size
    return (jnp.cos(angle), jnp.sin(angle))


def symbol_block(columns):
    freq = jnp.arange(M, dtype=jnp.int32)
    line = 4.0 * jnp.sin(jnp.pi * freq.astype(jnp.float32) / M) ** 2
    freq_y = columns // M
    freq_z = columns % M
    line_y = 4.0 * jnp.sin(jnp.pi * freq_y.astype(jnp.float32) / M) ** 2
    line_z = 4.0 * jnp.sin(jnp.pi * freq_z.astype(jnp.float32) / M) ** 2
    lam = line[:, None] + (line_y + line_z)[None, :]
    anchor = (freq[:, None] + freq_y[None, :] + freq_z[None, :] == 0).astype(jnp.float32)
    return (1.0 - anchor) / (K0 * float(M * M * M) * (lam + anchor))


def potential_solve(div, inverse, cosine, sine):
    real_part = along_cols(div, cosine, "z")
    imag_part = -along_cols(div, sine, "z")
    real_part, imag_part = (
        along_cols(real_part, cosine, "y") + along_cols(imag_part, sine, "y"),
        along_cols(imag_part, cosine, "y") - along_cols(real_part, sine, "y"),
    )
    joined = lax.all_to_all(
        jnp.stack([real_part, imag_part], 0), "sub", split_axis=3, concat_axis=2, tiled=True
    )
    real_part, imag_part = (joined[0], joined[1])
    real_part, imag_part = (
        along_planes(real_part, cosine) + along_planes(imag_part, sine),
        along_planes(imag_part, cosine) - along_planes(real_part, sine),
    )
    real_part = real_part * inverse[None]
    imag_part = imag_part * inverse[None]
    real_part, imag_part = (
        along_planes(real_part, cosine) - along_planes(imag_part, sine),
        along_planes(real_part, sine) + along_planes(imag_part, cosine),
    )
    joined = lax.all_to_all(
        jnp.stack([real_part, imag_part], 0), "sub", split_axis=2, concat_axis=3, tiled=True
    )
    real_part, imag_part = (joined[0], joined[1])
    real_part, imag_part = (
        along_cols(real_part, cosine, "y") - along_cols(imag_part, sine, "y"),
        along_cols(real_part, sine, "y") + along_cols(imag_part, cosine, "y"),
    )
    return along_cols(real_part, cosine, "z") - along_cols(imag_part, sine, "z")


def cell_strains(phi, units, last_z):
    following = passed_along(phi[:, :1], "sub", -1)
    grad_x = jnp.concatenate([phi[:, 1:], following], 1) - phi
    grad_y = jnp.roll(phi, -M, axis=2) - phi
    next_z = jnp.where(last_z, jnp.roll(phi, M - 1, axis=2), jnp.roll(phi, -1, axis=2))
    grad_z = next_z - phi
    return [units[:, i][:, None, None] + grads for i, grads in enumerate((grad_x, grad_y, grad_z))]


def micro_body(phase, soften, strain):
    planes = phase.shape[1]
    cond = phase[0] / (1.0 + soften[0] * jnp.sum(strain * strain))
    col_block = M * M // lax.axis_size("sub")
    columns = lax.axis_index("sub") * col_block + jnp.arange(col_block, dtype=jnp.int32)
    inverse = symbol_block(columns)
    cosine, sine = tables_for(M)
    units = jnp.eye(3, dtype=jnp.float32)
    col_z = jnp.arange(M * M, dtype=jnp.int32) % M
    last_z = col_z == M - 1
    first_z = col_z == 0
    phi = jnp.zeros((3, planes, M * M), jnp.float32)
    for sweep in range(MITERS):
        parts = cell_strains(phi, units, last_z)
        tau = [(cond - K0) * parts[i] for i in range(3)]
        previous = passed_along(tau[0][:, -1:], "sub", 1)
        div = tau[0] - jnp.concatenate([previous, tau[0][:, :-1]], 1)
        div = div + tau[1] - jnp.roll(tau[1], M, axis=2)
        prior_z = jnp.where(first_z, jnp.roll(tau[2], 1 - M, axis=2), jnp.roll(tau[2], 1, axis=2))
        div = div + tau[2] - prior_z
        phi = potential_solve(div, inverse, cosine, sine)
    parts = cell_strains(phi, units, last_z)
    sums = jnp.stack([jnp.sum(cond[None] * parts[i], axis=(1, 2)) for i in range(3)])
    table = lax.psum(sums, "sub") / float(M * M * M)
    return 0.5 * (table + table.T)


def residual_total(residual):
    return lax.psum(jnp.sum(residual * residual), ("grp", "sub"))


def body(displacement, load, kl_coef, damaged, owner, phase, soften):
    rows_x, rows_y, rows_z = displacement.shape
    grp_index = lax.axis_index("grp")
    sub_index = lax.axis_index("sub")
    total_x = rows_x * lax.axis_size("grp")
    total_y = rows_y * lax.axis_size("sub")
    coord_x = grp_index * rows_x - 1 + jnp.arange(rows_x + 1, dtype=jnp.int32)
    coord_y = sub_index * rows_y - 1 + jnp.arange(rows_y + 1, dtype=jnp.int32)
    coord_z = jnp.arange(rows_z, dtype=jnp.int32)
    inside = ((coord_x >= 0)[:, None, None] & (coord_y >= 0)[None, :, None]).astype(jnp.float32)
    kpad = conductivity(kl_coef, coord_x, coord_y, coord_z, total_x, total_y, rows_z) * inside
    point_z = damaged % rows_z
    rest = damaged // rows_z
    local_x = rest // total_y - grp_index * rows_x + 1
    local_y = rest % total_y - sub_index * rows_y + 1
    in_flux = (local_x >= 0) & (local_x <= rows_x) & (local_y >= 0) & (local_y <= rows_y)
    in_cells = (local_x >= 1) & (local_x <= rows_x) & (local_y >= 1) & (local_y <= rows_y)
    flat = (
        jnp.clip(local_x, 0, rows_x) * (rows_y + 1) + jnp.clip(local_y, 0, rows_y)
    ) * rows_z + point_z
    region = (rows_x + 1) * (rows_y + 1) * rows_z
    target = jnp.where(in_flux, flat, region)
    grads_u = padded_gradient(displacement)
    strains = point_values(grads_u, flat, in_cells)
    select = (owner == grp_index).astype(jnp.float32)
    rve_strain = jnp.sum(select[:, None] * strains, axis=0)
    tangent = micro_body(phase, soften, rve_strain)
    tangents = lax.all_gather(tangent.reshape(1, 9), "grp", axis=0, tiled=True)
    tensors = tangents[owner].reshape(-1, 3, 3)
    rhs = load - divergence(grads_u, displacement, kpad, tensors, flat, target)
    step_field = jnp.zeros_like(rhs)
    residual = rhs
    direction = rhs
    norm_now = residual_total(residual)
    for sweep in range(CG_ITERS):
        image = divergence(padded_gradient(direction), direction, kpad, tensors, flat, target)
        alpha = norm_now / lax.psum(jnp.sum(direction * image), ("grp", "sub"))
        step_field = step_field + alpha * direction
        residual = residual - alpha * image
        norm_next = residual_total(residual)
        direction = residual + norm_next / norm_now * direction
        norm_now = norm_next
    step_grads = point_values(padded_gradient(step_field), flat, in_cells)
    point_flux = jnp.einsum("pij,pj->pi", tensors, step_grads, precision=HIGH)
    return (step_field, residual, tangents, point_flux)


def solution(mesh):
    return jax.shard_map(
        body,
        mesh=mesh,
        in_specs=(
            P("grp", "sub", None),
            P("grp", "sub", None),
            P(),
            P(),
            P(),
            P("grp", "sub", None),
            P("grp", "sub", None),
        ),
        out_specs=(P("grp", "sub", None), P("grp", "sub", None), P(), P()),
        check_vma=False,
    )
```

profile of v0, /device:TPU:0, one launch (start us, length us, event | category | flops | bytes accessed | tf_op | source)
XLA Modules:
  0.0 2055.8 jit_solution(18226921929787480789)
XLA Ops:
  23.7 10.2 copy.503
  41.8 41.8 %psum.105 = f32[16,3]{1,0:T(8,128)S(1)} all-reduce(f32[16,3]{1,0:T(8,128)S(1)} %fusion.237), channel_id=1, replica_groups=mesh['grp'=16,'sub'=2] {'grp','sub'}, use_global_device_ids=true, to_apply=%region_0.1 | all-reduce | flops 48 | bytes 384 | tf_op jit(solution)/shard_map/psum | solution.py:52
  390.6 10.8 copy.586
  406.5 20.8 %all-gather = f32[16,1,9]{2,1,0:T(1,128)S(1)} all-gather(f32[1,1,9]{2,1,0:T(1,128)S(1)} %reshape.847), channel_id=1, replica_groups=mesh['grp'=16,'sub'=2] {'grp'}, dimensions={0}, use_global_device_ids=true | all-gather | bytes 612 | tf_op jit(solution)/shard_map/all_gather | solution.py:199
  428.3 14.0 scatter_fusion
  442.3 52.6 %fusion.696 = (f32[1,8,16,256]{0,3,2,1:T(8,128)}, f32[1,8,16,256]{0,3,2,1:T(8,128)}, f32[1,8,16,256]{0,3,2,1:T(8,128)}, f32[1,8,16,256]{0,3,2,1:T(8,128)}, f32[1,8,16,256]{0,3,2,1:T(8,128)}) fusion(f32[3,9,17,256]{0,3,2,1:T(8,128)} %bitcast.662), kind=kLoop, calls=%fused_computation.898 | loop fusion | bytes 1310720 | tf_op jit(solution)/shard_map/slice | solution.py:63
  524.8 10.0 copy.788
  560.9 10.2 copy.592
  578.6 10.2 copy.593
  588.8 14.0 scatter_fusion.1
  602.9 52.8 %fusion.695 = (f32[1,8,16,256]{0,3,2,1:T(8,128)}, f32[1,8,16,256]{0,3,2,1:T(8,128)}, f32[1,8,16,256]{0,3,2,1:T(8,128)}, f32[1,8,16,256]{0,3,2,1:T(8,128)}, f32[1,8,16,256]{0,3,2,1:T(8,128)}) fusion(f32[3,9,17,256]{0,3,2,1:T(8,128)} %bitcast.664), kind=kLoop, calls=%fused_computation.897 | loop fusion | bytes 1310720 | tf_op jit(solution)/shard_map/slice | solution.py:63
  665.6 9.9 copy.795
  695.4 9.9 copy.791
  706.1 39.2 %all-reduce.19 = (f32[]{:T(128)}, f32[]{:T(128)}) all-reduce(f32[]{:T(128)} %get-tuple-element.8, f32[]{:T(128)} %get-tuple-element.7), channel_id=1, replica_groups=mesh['grp'=16,'sub'=2] {'grp','sub'}, use_global_device_ids=true, to_apply=%region_9.10 | all-reduce | flops 2 | bytes 16 | tf_op jit(solution)/shard_map/psum | solution.py:169
  747.3 40.9 %psum.109 = f32[]{:T(128)} all-reduce(f32[]{:T(128)} %multiply_reduce_fusion.11), channel_id=1, replica_groups=mesh['grp'=16,'sub'=2] {'grp','sub'}, use_global_device_ids=true, to_apply=%region_14.15 | all-reduce | flops 1 | bytes 8 | tf_op jit(solution)/shard_map/psum | solution.py:169
  805.5 10.2 copy.599
  823.3 10.2 copy.600
  833.5 14.0 scatter_fusion.2
  847.6 52.8 %fusion.694 = (f32[1,8,16,256]{0,3,2,1:T(8,128)}, f32[1,8,16,256]{0,3,2,1:T(8,128)}, f32[1,8,16,256]{0,3,2,1:T(8,128)}, f32[1,8,16,256]{0,3,2,1:T(8,128)}, f32[1,8,16,256]{0,3,2,1:T(8,128)}) fusion(f32[3,9,17,256]{0,3,2,1:T(8,128)} %bitcast.665), kind=kLoop, calls=%fused_computation.896 | loop fusion | bytes 1310720 | tf_op jit(solution)/shard_map/slice | solution.py:63
  930.2 9.9 copy.798
  950.8 40.7 %psum.110 = f32[]{:T(128)} all-reduce(f32[]{:T(128)} %get-tuple-element.27), channel_id=1, replica_groups=mesh['grp'=16,'sub'=2] {'grp','sub'}, use_global_device_ids=true, to_apply=%region_17.18 | all-reduce | flops 1 | bytes 8 | tf_op jit(solution)/shard_map/psum | solution.py:208
  993.5 40.1 %psum.111 = f32[]{:T(128)} all-reduce(f32[]{:T(128)} %get-tuple-element.25), channel_id=1, replica_groups=mesh['grp'=16,'sub'=2] {'grp','sub'}, use_global_device_ids=true, to_apply=%region_19.20 | all-reduce | flops 1 | bytes 8 | tf_op jit(solution)/shard_map/psum | solution.py:169
  1052.3 10.2 copy.606
  1070.0 10.2 copy.607
  1080.2 14.0 scatter_fusion.3
  1094.3 53.1 %fusion.693 = (f32[1,8,16,256]{0,3,2,1:T(8,128)}, f32[1,8,16,256]{0,3,2,1:T(8,128)}, f32[1,8,16,256]{0,3,2,1:T(8,128)}, f32[1,8,16,256]{0,3,2,1:T(8,128)}, f32[1,8,16,256]{0,3,2,1:T(8,128)}) fusion(f32[3,9,17,256]{0,3,2,1:T(8,128)} %bitcast.666), kind=kLoop, calls=%fused_computation.895 | loop fusion | bytes 1310720 | tf_op jit(solution)/shard_map/slice | solution.py:63
  1197.8 40.4 %psum.112 = f32[]{:T(128)} all-reduce(f32[]{:T(128)} %get-tuple-element.23), channel_id=1, replica_groups=mesh['grp'=16,'sub'=2] {'grp','sub'}, use_global_device_ids=true, to_apply=%region_22.23 | all-reduce | flops 1 | bytes 8 | tf_op jit(solution)/shard_map/psum | solution.py:208
  1240.1 40.2 %psum.113 = f32[]{:T(128)} all-reduce(f32[]{:T(128)} %get-tuple-element.21), channel_id=1, replica_groups=mesh['grp'=16,'sub'=2] {'grp','sub'}, use_global_device_ids=true, to_apply=%region_24.25 | all-reduce | flops 1 | bytes 8 | tf_op jit(solution)/shard_map/psum | solution.py:169
  1298.3 10.2 copy.613
  1316.0 10.2 copy.614
  1326.3 14.0 scatter_fusion.4
  1340.3 52.8 %fusion.692 = (f32[1,8,16,256]{0,3,2,1:T(8,128)}, f32[1,8,16,256]{0,3,2,1:T(8,128)}, f32[1,8,16,256]{0,3,2,1:T(8,128)}, f32[1,8,16,256]{0,3,2,1:T(8,128)}, f32[1,8,16,256]{0,3,2,1:T(8,128)}) fusion(f32[3,9,17,256]{0,3,2,1:T(8,128)} %bitcast.667), kind=kLoop, calls=%fused_computation.894 | loop fusion | bytes 1310720 | tf_op jit(solution)/shard_map/slice | solution.py:63
  1443.5 40.7 %psum.114 = f32[]{:T(128)} all-reduce(f32[]{:T(128)} %get-tuple-element.19), channel_id=1, replica_groups=mesh['grp'=16,'sub'=2] {'grp','sub'}, use_global_device_ids=true, to_apply=%region_27.28 | all-reduce | flops 1 | bytes 8 | tf_op jit(solution)/shard_map/psum | solution.py:208
  1486.2 39.9 %psum.115 = f32[]{:T(128)} all-reduce(f32[]{:T(128)} %get-tuple-element.17), channel_id=1, replica_groups=mesh['grp'=16,'sub'=2] {'grp','sub'}, use_global_device_ids=true, to_apply=%region_29.30 | all-reduce | flops 1 | bytes 8 | tf_op jit(solution)/shard_map/psum | solution.py:169
  1545.0 10.2 copy.620
  1562.7 10.2 copy.621
  1572.9 14.0 scatter_fusion.5
  1587.0 52.8 %fusion.691 = (f32[1,8,16,256]{0,3,2,1:T(8,128)}, f32[1,8,16,256]{0,3,2,1:T(8,128)}, f32[1,8,16,256]{0,3,2,1:T(8,128)}, f32[1,8,16,256]{0,3,2,1:T(8,128)}, f32[1,8,16,256]{0,3,2,1:T(8,128)}) fusion(f32[3,9,17,256]{0,3,2,1:T(8,128)} %bitcast.668), kind=kLoop, calls=%fused_computation.893 | loop fusion | bytes 1310720 | tf_op jit(solution)/shard_map/slice | solution.py:63
  1690.2 40.4 %psum.116 = f32[]{:T(128)} all-reduce(f32[]{:T(128)} %get-tuple-element.15), channel_id=1, replica_groups=mesh['grp'=16,'sub'=2] {'grp','sub'}, use_global_device_ids=true, to_apply=%region_32.33 | all-reduce | flops 1 | bytes 8 | tf_op jit(solution)/shard_map/psum | solution.py:208
  1732.6 40.2 %psum.117 = f32[]{:T(128)} all-reduce(f32[]{:T(128)} %get-tuple-element.13), channel_id=1, replica_groups=mesh['grp'=16,'sub'=2] {'grp','sub'}, use_global_device_ids=true, to_apply=%region_34.35 | all-reduce | flops 1 | bytes 8 | tf_op jit(solution)/shard_map/psum | solution.py:169
  1790.8 10.2 copy.627
  1808.5 10.2 copy.628
  1818.8 14.0 scatter_fusion.6
  1832.8 52.8 %fusion.690 = (f32[1,8,16,256]{0,3,2,1:T(8,128)}, f32[1,8,16,256]{0,3,2,1:T(8,128)}, f32[1,8,16,256]{0,3,2,1:T(8,128)}, f32[1,8,16,256]{0,3,2,1:T(8,128)}, f32[1,8,16,256]{0,3,2,1:T(8,128)}) fusion(f32[3,9,17,256]{0,3,2,1:T(8,128)} %bitcast.663), kind=kLoop, calls=%fused_computation.892 | loop fusion | bytes 1310720 | tf_op jit(solution)/shard_map/slice | solution.py:63
  1915.5 10.0 copy.818
  1936.2 40.6 %psum.118 = f32[]{:T(128)} all-reduce(f32[]{:T(128)} %get-tuple-element.11), channel_id=1, replica_groups=mesh['grp'=16,'sub'=2] {'grp','sub'}, use_global_device_ids=true, to_apply=%region_37.38 | all-reduce | flops 1 | bytes 8 | tf_op jit(solution)/shard_map/psum | solution.py:208
  1995.3 10.2 copy.634
  2012.9 41.3 %psum.119 = f32[16,3]{1,0:T(8,128)S(1)} all-reduce(f32[16,3]{1,0:T(8,128)S(1)} %broadcast_select_fusion), channel_id=1, replica_groups=mesh['grp'=16,'sub'=2] {'grp','sub'}, use_global_device_ids=true, to_apply=%region_38.39 | all-reduce | flops 48 | bytes 384 | tf_op jit(solution)/shard_map/psum | solution.py:52
  (615 shorter events, 818.4 us)
Async XLA Ops:
  0.7 84.9 %collective-permute-start.4 = (f32[3,1,1024]{2,1,0:T(1,128)S(1)}, f32[3,1,1024]{2,1,0:T(1,128)S(1)}, u32[]{:S(2)}, u32[]{:S(2)}) collective-permute-start(f32[3,1,1024]{2,1,0:T(1,128)S(1)} %slice.710), channel_id=1, source_target_pairs={{0,1},{1,0},{2,3},{3,2},{4,5},{5,4},{6,7},{7,6},{8,9},{9,8},{10,11... | collective-permute-start | bytes 36872 | tf_op jit(solution)/shard_map/ppermute | solution.py:29
  4.4 10.0 collective-permute-start.1
  5.7 7.7 collective-permute-start
  14.5 6.0 collective-permute-start.3
  15.8 5.9 collective-permute-start.2
  86.4 4.0 collective-permute-start.5
  106.7 9.5 all-to-all-start
  147.8 3.8 collective-permute-start.6
  154.1 10.8 collective-permute-start.7
  227.2 3.8 collective-permute-start.8
  233.4 10.1 collective-permute-start.9
  306.0 3.8 collective-permute-start.10
  312.2 9.4 collective-permute-start.11
  341.7 9.3 all-to-all-start.6
  368.3 9.3 all-to-all-start.7
  384.8 3.8 collective-permute-start.12
  544.9 448.0 %copy-start = (f32[8,16,256]{2,1,0:T(8,128)}, f32[8,16,256]{2,1,0:T(8,128)S(1)}, u32[]{:S(2)}) copy-start(f32[8,16,256]{2,1,0:T(8,128)S(1)} %fusion.102) | copy-start | bytes 393220
  544.9 3.6 collective-permute-start.13
  547.1 3.1 collective-permute-start.14
  550.2 5.3 collective-permute-start.15
  554.2 5.6 collective-permute-start.16
  789.6 245.3 %copy-start.4 = (f32[8,16,256]{2,1,0:T(8,128)}, f32[8,16,256]{2,1,0:T(8,128)S(1)}, u32[]{:S(2)}) copy-start(f32[8,16,256]{2,1,0:T(8,128)S(1)} %multiply_add_fusion.5) | copy-start | bytes 393220
  789.6 2.6 collective-permute-start.17
  790.9 5.8 collective-permute-start.18
  796.7 3.5 collective-permute-start.19
  798.8 5.6 collective-permute-start.20
  1034.9 246.7 %copy-start.6 = (f32[8,16,256]{2,1,0:T(8,128)}, f32[8,16,256]{2,1,0:T(8,128)S(1)}, u32[]{:S(2)}) copy-start(f32[8,16,256]{2,1,0:T(8,128)S(1)} %multiply_add_fusion.4) | copy-start | bytes 393220
  1034.9 2.6 collective-permute-start.21
  1036.2 5.8 collective-permute-start.22
  1042.0 4.9 collective-permute-start.23
  1045.6 5.6 collective-permute-start.24
  1281.7 245.7 %copy-start.8 = (f32[8,16,256]{2,1,0:T(8,128)}, f32[8,16,256]{2,1,0:T(8,128)S(1)}, u32[]{:S(2)}) copy-start(f32[8,16,256]{2,1,0:T(8,128)S(1)} %multiply_add_fusion.3) | copy-start | bytes 393220
  1281.7 2.6 collective-permute-start.25
  1283.0 5.8 collective-permute-start.26
  1288.8 4.2 collective-permute-start.27
  1291.6 5.6 collective-permute-start.28
  1527.5 2.6 collective-permute-start.29
  1528.8 5.8 collective-permute-start.30
  1534.6 5.1 collective-permute-start.31
  1538.3 5.6 collective-permute-start.32
  1774.1 2.6 collective-permute-start.33
  1775.4 5.8 collective-permute-start.34
  1781.2 4.3 collective-permute-start.35
  1784.1 5.6 collective-permute-start.36
  1978.3 2.6 collective-permute-start.37
  1979.6 5.8 collective-permute-start.38
  1985.4 4.7 collective-permute-start.39
  1988.8 5.6 collective-permute-start.40
  (31 other events, 1716.0 us)
where the time goes:
time: 2070 us; the launch traced here: 2060 us
  local copies, waits for them, and re-layouts  1160 us (56%)
  blocking collectives  596 us (29%)
  waiting for transfers between devices  82.4 us (4%)
  starting transfers between devices  76.9 us (4%)
  matrix products  60.3 us (3%)
  other arithmetic  57.4 us (3%)
    unnamed x118, local copies, waits for them, and re-layouts  392 us
    slice x7, local copies, waits for them, and re-layouts, divergence(): flux[0, 1:, 1:]  370 us
    psum x6, blocking collectives, residual_total(): return lax.psum(jnp.sum(residual * residual), ('grp', 'sub'))  240 us
    psum x5, blocking collectives, body(): alpha = norm_now / lax.psum(jnp.sum(direction * image), ('grp', 'sub'))  203 us
    scatter x7, local copies, waits for them, and re-layouts, divergence(): flux.reshape(3, -1).at[:, target].set(newval, mode='drop')  98.3 us
    another operation x32, local copies, waits for them, and re-layouts, padded_gradient(): jnp.stack([padded[1:, :-1] - center, padded[:-1, 1:] - center, beyond - c...  85.6 us
    psum x2, blocking collectives, point_values(): return lax.psum(local_part, ('grp', 'sub'))  83.1 us
    mul x8, local copies, waits for them, and re-layouts, divergence(): flux = kpad[None] * grads  72.2 us
  transfers between devices with their start and end apart: 44, of which 28 were waited for; matrix products, arithmetic and copies ran while one was open for 3% of the time, Pallas kernels for 0%

commit v1 on v0

--- a/solution.py
+++ b/solution.py
@@ -104,8 +104,16 @@
         along_cols(real_part, cosine, "y") + along_cols(imag_part, sine, "y"),
         along_cols(imag_part, cosine, "y") - along_cols(real_part, sine, "y"),
     )
-    joined = lax.all_to_all(
-        jnp.stack([real_part, imag_part], 0), "sub", split_axis=3, concat_axis=2, tiled=True
+    joined = jnp.concatenate(
+        lax.all_to_all(
+            jnp.stack(
+                jnp.split(jnp.stack([real_part, imag_part], 0), lax.axis_size("sub"), axis=3)
+            ),
+            "sub",
+            0,
+            0,
+        ),
+        axis=2,
     )
     real_part, imag_part = (joined[0], joined[1])
     real_part, imag_part = (

time: 2070 us -> 1980 us (0.957)
  local copies, waits for them, and re-layouts: 1160 us -> 1090 us
    unnamed x118 -> x116, local copies, waits for them, and re-layouts: 392 us -> 350 us
where the time goes in v1:
time: 1980 us; the launch traced here: 1970 us
  local copies, waits for them, and re-layouts  1090 us (55%)
  blocking collectives  596 us (30%)
  waiting for transfers between devices  84.8 us (4%)
  starting transfers between devices  76.9 us (4%)
  matrix products  60.1 us (3%)
  other arithmetic  44 us (2%)
    slice x7, local copies, waits for them, and re-layouts, divergence(): flux[0, 1:, 1:]  370 us
    unnamed x116, local copies, waits for them, and re-layouts  350 us
    psum x6, blocking collectives, residual_total(): return lax.psum(jnp.sum(residual * residual), ('grp', 'sub'))  240 us
    psum x5, blocking collectives, body(): alpha = norm_now / lax.psum(jnp.sum(direction * image), ('grp', 'sub'))  203 us
    scatter x7, local copies, waits for them, and re-layouts, divergence(): flux.reshape(3, -1).at[:, target].set(newval, mode='drop')  99.8 us
    another operation x32, local copies, waits for them, and re-layouts, padded_gradient(): jnp.stack([padded[1:, :-1] - center, padded[:-1, 1:] - center, beyond - c...  85.4 us
    psum x2, blocking collectives, point_values(): return lax.psum(local_part, ('grp', 'sub'))  82.6 us
    mul x8, local copies, waits for them, and re-layouts, divergence(): flux = kpad[None] * grads  71.8 us
  transfers between devices with their start and end apart: 44, of which 28 were waited for; matrix products, arithmetic and copies ran while one was open for 3% of the time, Pallas kernels for 0%

profile of v1, /device:TPU:0, one launch (start us, length us, event | category | flops | bytes accessed | tf_op | source)
XLA Modules:
  0.0 1966.8 jit_solution(13915189382305955545)
XLA Ops:
  23.7 10.1 copy.507
  41.2 41.3 %psum.105 = f32[16,3]{1,0:T(8,128)S(1)} all-reduce(f32[16,3]{1,0:T(8,128)S(1)} %fusion.237), channel_id=1, replica_groups=mesh['grp'=16,'sub'=2] {'grp','sub'}, use_global_device_ids=true, to_apply=%region_0.1 | all-reduce | flops 48 | bytes 384 | tf_op jit(solution)/shard_map/psum | solution.py:52
  205.3 10.7 all_to_all.83
  300.7 10.6 copy.590
  316.4 20.5 %all-gather = f32[16,1,9]{2,1,0:T(1,128)S(1)} all-gather(f32[1,1,9]{2,1,0:T(1,128)S(1)} %reshape.867), channel_id=1, replica_groups=mesh['grp'=16,'sub'=2] {'grp'}, dimensions={0}, use_global_device_ids=true | all-gather | bytes 612 | tf_op jit(solution)/shard_map/all_gather | solution.py:207
  338.0 14.2 scatter_fusion
  352.1 52.8 %fusion.696 = (f32[1,8,16,256]{0,3,2,1:T(8,128)}, f32[1,8,16,256]{0,3,2,1:T(8,128)}, f32[1,8,16,256]{0,3,2,1:T(8,128)}, f32[1,8,16,256]{0,3,2,1:T(8,128)}, f32[1,8,16,256]{0,3,2,1:T(8,128)}) fusion(f32[3,9,17,256]{0,3,2,1:T(8,128)} %bitcast.666), kind=kLoop, calls=%fused_computation.914 | loop fusion | bytes 1310720 | tf_op jit(solution)/shard_map/slice | solution.py:63
  424.8 9.9 copy.793
  434.8 10.0 copy.792
  444.8 9.9 copy.790
  470.9 10.2 copy.596
  488.6 10.2 copy.597
  498.8 14.2 scatter_fusion.1
  513.0 52.8 %fusion.695 = (f32[1,8,16,256]{0,3,2,1:T(8,128)}, f32[1,8,16,256]{0,3,2,1:T(8,128)}, f32[1,8,16,256]{0,3,2,1:T(8,128)}, f32[1,8,16,256]{0,3,2,1:T(8,128)}, f32[1,8,16,256]{0,3,2,1:T(8,128)}) fusion(f32[3,9,17,256]{0,3,2,1:T(8,128)} %bitcast.668), kind=kLoop, calls=%fused_computation.913 | loop fusion | bytes 1310720 | tf_op jit(solution)/shard_map/slice | solution.py:63
  616.2 39.2 %all-reduce.19 = (f32[]{:T(128)}, f32[]{:T(128)}) all-reduce(f32[]{:T(128)} %get-tuple-element.8, f32[]{:T(128)} %get-tuple-element.7), channel_id=1, replica_groups=mesh['grp'=16,'sub'=2] {'grp','sub'}, use_global_device_ids=true, to_apply=%region_9.10 | all-reduce | flops 2 | bytes 16 | tf_op jit(solution)/shard_map/psum | solution.py:177
  657.5 40.9 %psum.109 = f32[]{:T(128)} all-reduce(f32[]{:T(128)} %multiply_reduce_fusion.11), channel_id=1, replica_groups=mesh['grp'=16,'sub'=2] {'grp','sub'}, use_global_device_ids=true, to_apply=%region_14.15 | all-reduce | flops 1 | bytes 8 | tf_op jit(solution)/shard_map/psum | solution.py:177
  715.7 10.2 copy.603
  733.4 10.2 copy.604
  743.6 14.3 scatter_fusion.2
  757.9 52.8 %fusion.694 = (f32[1,8,16,256]{0,3,2,1:T(8,128)}, f32[1,8,16,256]{0,3,2,1:T(8,128)}, f32[1,8,16,256]{0,3,2,1:T(8,128)}, f32[1,8,16,256]{0,3,2,1:T(8,128)}, f32[1,8,16,256]{0,3,2,1:T(8,128)}) fusion(f32[3,9,17,256]{0,3,2,1:T(8,128)} %bitcast.669), kind=kLoop, calls=%fused_computation.912 | loop fusion | bytes 1310720 | tf_op jit(solution)/shard_map/slice | solution.py:63
  861.1 40.7 %psum.110 = f32[]{:T(128)} all-reduce(f32[]{:T(128)} %get-tuple-element.27), channel_id=1, replica_groups=mesh['grp'=16,'sub'=2] {'grp','sub'}, use_global_device_ids=true, to_apply=%region_17.18 | all-reduce | flops 1 | bytes 8 | tf_op jit(solution)/shard_map/psum | solution.py:216
  903.8 40.1 %psum.111 = f32[]{:T(128)} all-reduce(f32[]{:T(128)} %get-tuple-element.25), channel_id=1, replica_groups=mesh['grp'=16,'sub'=2] {'grp','sub'}, use_global_device_ids=true, to_apply=%region_19.20 | all-reduce | flops 1 | bytes 8 | tf_op jit(solution)/shard_map/psum | solution.py:177
  962.6 10.2 copy.610
  980.3 10.2 copy.611
  990.5 14.5 scatter_fusion.3
  1005.0 52.8 %fusion.693 = (f32[1,8,16,256]{0,3,2,1:T(8,128)}, f32[1,8,16,256]{0,3,2,1:T(8,128)}, f32[1,8,16,256]{0,3,2,1:T(8,128)}, f32[1,8,16,256]{0,3,2,1:T(8,128)}, f32[1,8,16,256]{0,3,2,1:T(8,128)}) fusion(f32[3,9,17,256]{0,3,2,1:T(8,128)} %bitcast.670), kind=kLoop, calls=%fused_computation.911 | loop fusion | bytes 1310720 | tf_op jit(solution)/shard_map/slice | solution.py:63
  1108.2 40.4 %psum.112 = f32[]{:T(128)} all-reduce(f32[]{:T(128)} %get-tuple-element.23), channel_id=1, replica_groups=mesh['grp'=16,'sub'=2] {'grp','sub'}, use_global_device_ids=true, to_apply=%region_22.23 | all-reduce | flops 1 | bytes 8 | tf_op jit(solution)/shard_map/psum | solution.py:216
  1150.6 40.2 %psum.113 = f32[]{:T(128)} all-reduce(f32[]{:T(128)} %get-tuple-element.21), channel_id=1, replica_groups=mesh['grp'=16,'sub'=2] {'grp','sub'}, use_global_device_ids=true, to_apply=%region_24.25 | all-reduce | flops 1 | bytes 8 | tf_op jit(solution)/shard_map/psum | solution.py:177
  1208.7 10.2 copy.617
  1226.4 10.2 copy.618
  1236.6 14.2 scatter_fusion.4
  1250.8 52.8 %fusion.692 = (f32[1,8,16,256]{0,3,2,1:T(8,128)}, f32[1,8,16,256]{0,3,2,1:T(8,128)}, f32[1,8,16,256]{0,3,2,1:T(8,128)}, f32[1,8,16,256]{0,3,2,1:T(8,128)}, f32[1,8,16,256]{0,3,2,1:T(8,128)}) fusion(f32[3,9,17,256]{0,3,2,1:T(8,128)} %bitcast.671), kind=kLoop, calls=%fused_computation.910 | loop fusion | bytes 1310720 | tf_op jit(solution)/shard_map/slice | solution.py:63
  1354.0 40.7 %psum.114 = f32[]{:T(128)} all-reduce(f32[]{:T(128)} %get-tuple-element.19), channel_id=1, replica_groups=mesh['grp'=16,'sub'=2] {'grp','sub'}, use_global_device_ids=true, to_apply=%region_27.28 | all-reduce | flops 1 | bytes 8 | tf_op jit(solution)/shard_map/psum | solution.py:216
  1396.8 39.9 %psum.115 = f32[]{:T(128)} all-reduce(f32[]{:T(128)} %get-tuple-element.17), channel_id=1, replica_groups=mesh['grp'=16,'sub'=2] {'grp','sub'}, use_global_device_ids=true, to_apply=%region_29.30 | all-reduce | flops 1 | bytes 8 | tf_op jit(solution)/shard_map/psum | solution.py:177
  1455.5 10.2 copy.624
  1473.3 10.2 copy.625
  1483.5 14.2 scatter_fusion.5
  1497.7 52.8 %fusion.691 = (f32[1,8,16,256]{0,3,2,1:T(8,128)}, f32[1,8,16,256]{0,3,2,1:T(8,128)}, f32[1,8,16,256]{0,3,2,1:T(8,128)}, f32[1,8,16,256]{0,3,2,1:T(8,128)}, f32[1,8,16,256]{0,3,2,1:T(8,128)}) fusion(f32[3,9,17,256]{0,3,2,1:T(8,128)} %bitcast.672), kind=kLoop, calls=%fused_computation.909 | loop fusion | bytes 1310720 | tf_op jit(solution)/shard_map/slice | solution.py:63
  1600.9 40.4 %psum.116 = f32[]{:T(128)} all-reduce(f32[]{:T(128)} %get-tuple-element.15), channel_id=1, replica_groups=mesh['grp'=16,'sub'=2] {'grp','sub'}, use_global_device_ids=true, to_apply=%region_32.33 | all-reduce | flops 1 | bytes 8 | tf_op jit(solution)/shard_map/psum | solution.py:216
  1643.3 40.2 %psum.117 = f32[]{:T(128)} all-reduce(f32[]{:T(128)} %get-tuple-element.13), channel_id=1, replica_groups=mesh['grp'=16,'sub'=2] {'grp','sub'}, use_global_device_ids=true, to_apply=%region_34.35 | all-reduce | flops 1 | bytes 8 | tf_op jit(solution)/shard_map/psum | solution.py:177
  1701.5 10.2 copy.631
  1719.2 10.2 copy.632
  1729.4 14.3 scatter_fusion.6
  1743.7 52.8 %fusion.690 = (f32[1,8,16,256]{0,3,2,1:T(8,128)}, f32[1,8,16,256]{0,3,2,1:T(8,128)}, f32[1,8,16,256]{0,3,2,1:T(8,128)}, f32[1,8,16,256]{0,3,2,1:T(8,128)}, f32[1,8,16,256]{0,3,2,1:T(8,128)}) fusion(f32[3,9,17,256]{0,3,2,1:T(8,128)} %bitcast.667), kind=kLoop, calls=%fused_computation.908 | loop fusion | bytes 1310720 | tf_op jit(solution)/shard_map/slice | solution.py:63
  1826.4 10.0 copy.822
  1847.0 40.6 %psum.118 = f32[]{:T(128)} all-reduce(f32[]{:T(128)} %get-tuple-element.11), channel_id=1, replica_groups=mesh['grp'=16,'sub'=2] {'grp','sub'}, use_global_device_ids=true, to_apply=%region_37.38 | all-reduce | flops 1 | bytes 8 | tf_op jit(solution)/shard_map/psum | solution.py:216
  1906.2 10.2 copy.638
  1923.7 41.3 %psum.119 = f32[16,3]{1,0:T(8,128)S(1)} all-reduce(f32[16,3]{1,0:T(8,128)S(1)} %broadcast_select_fusion), channel_id=1, replica_groups=mesh['grp'=16,'sub'=2] {'grp','sub'}, use_global_device_ids=true, to_apply=%region_38.39 | all-reduce | flops 48 | bytes 384 | tf_op jit(solution)/shard_map/psum | solution.py:52
  (616 shorter events, 728.3 us)
Async XLA Ops:
  0.7 83.2 %collective-permute-start.4 = (f32[3,1,1024]{2,1,0:T(1,128)S(1)}, f32[3,1,1024]{2,1,0:T(1,128)S(1)}, u32[]{:S(2)}, u32[]{:S(2)}) collective-permute-start(f32[3,1,1024]{2,1,0:T(1,128)S(1)} %slice.710), channel_id=1, source_target_pairs={{0,1},{1,0},{2,3},{3,2},{4,5},{5,4},{6,7},{7,6},{8,9},{9,8},{10,11... | collective-permute-start | bytes 36872 | tf_op jit(solution)/shard_map/ppermute | solution.py:29
  4.4 9.9 collective-permute-start.1
  5.7 7.7 collective-permute-start
  14.4 6.0 collective-permute-start.3
  15.7 5.9 collective-permute-start.2
  84.6 4.0 collective-permute-start.5
  96.1 9.8 all-to-all-start
  124.9 3.8 collective-permute-start.6
  130.3 9.9 collective-permute-start.7
  178.7 3.8 collective-permute-start.8
  184.8 9.8 collective-permute-start.9
  235.1 3.8 collective-permute-start.10
  241.2 9.9 collective-permute-start.11
  262.3 10.9 all-to-all-start.6
  278.0 9.7 all-to-all-start.7
  294.9 3.8 collective-permute-start.12
  454.9 448.2 %copy-start = (f32[8,16,256]{2,1,0:T(8,128)}, f32[8,16,256]{2,1,0:T(8,128)S(1)}, u32[]{:S(2)}) copy-start(f32[8,16,256]{2,1,0:T(8,128)S(1)} %fusion.102) | copy-start | bytes 393220
  454.9 3.6 collective-permute-start.13
  457.1 3.1 collective-permute-start.14
  460.2 5.3 collective-permute-start.15
  464.2 5.6 collective-permute-start.16
  699.7 245.4 %copy-start.4 = (f32[8,16,256]{2,1,0:T(8,128)}, f32[8,16,256]{2,1,0:T(8,128)S(1)}, u32[]{:S(2)}) copy-start(f32[8,16,256]{2,1,0:T(8,128)S(1)} %multiply_add_fusion.5) | copy-start | bytes 393220
  699.8 2.6 collective-permute-start.17
  701.1 5.8 collective-permute-start.18
  706.9 3.5 collective-permute-start.19
  709.0 5.6 collective-permute-start.20
  945.2 246.9 %copy-start.6 = (f32[8,16,256]{2,1,0:T(8,128)}, f32[8,16,256]{2,1,0:T(8,128)S(1)}, u32[]{:S(2)}) copy-start(f32[8,16,256]{2,1,0:T(8,128)S(1)} %multiply_add_fusion.4) | copy-start | bytes 393220
  945.2 2.6 collective-permute-start.21
  946.5 5.8 collective-permute-start.22
  952.3 4.9 collective-permute-start.23
  955.9 5.6 collective-permute-start.24
  1192.1 245.9 %copy-start.8 = (f32[8,16,256]{2,1,0:T(8,128)}, f32[8,16,256]{2,1,0:T(8,128)S(1)}, u32[]{:S(2)}) copy-start(f32[8,16,256]{2,1,0:T(8,128)S(1)} %multiply_add_fusion.3) | copy-start | bytes 393220
  1192.1 2.6 collective-permute-start.25
  1193.4 5.8 collective-permute-start.26
  1199.2 4.2 collective-permute-start.27
  1202.0 5.6 collective-permute-start.28
  1438.0 2.6 collective-permute-start.29
  1439.3 5.8 collective-permute-start.30
  1445.1 5.1 collective-permute-start.31
  1448.9 5.6 collective-permute-start.32
  1684.9 2.6 collective-permute-start.33
  1686.1 5.8 collective-permute-start.34
  1691.9 4.3 collective-permute-start.35
  1694.8 5.6 collective-permute-start.36
  1889.1 2.6 collective-permute-start.37
  1890.4 5.8 collective-permute-start.38
  1896.2 4.7 collective-permute-start.39
  1899.7 5.6 collective-permute-start.40
  (32 other events, 1661.5 us)
